TPU v7x, 256 devices: a whole 4x4x8 slice. The times are simulated.
256 devices in a mesh: gx: 16 (over z, core), gy: 16 (over x, y).
Axes of the slice: x: 4, y: 4, z: 8, core: 2. Of those that a mesh axis runs over, the one named last changes fastest.
Arguments:
- right_sides: float32 [16384, 8, 128], P(('gx', 'gy')), may hold values from -30 to 30
- diag_blocks: bfloat16 [16384, 128, 128], P(('gx', 'gy')), may hold values from -1 to 2
- face_blocks: bfloat16 [16384, 4, 128, 128], P(('gx', 'gy')), may hold values from -0.125 to 0.125
- neighbours: int32 [16384, 4], P(('gx', 'gy')), may hold values from -1 to 207, as said below
- send_slots: int32 [256, 9, 16], P(('gx', 'gy')), may hold values from -1 to 63, as said below
- counts: int32 [256], P(('gx', 'gy')), may hold values from 32 to 64, as said below
Outputs:
- solution: float32 [16384, 8, 128], P(('gx', 'gy'))
- residual: float32 [16384, 8, 128], P(('gx', 'gy'))
Inputs may be any that keep to these rules, and one draw needn't show every extreme that they name: The first counts[g] slots of group g hold its elements; some group has exactly 64. send_slots[g, d, k] is a live slot of group g whose vector group g sends, as its k-th ghost of direction d = 3 (dx + 1) + (dy + 1), to the group at grid offset (dx, dy); -1 marks no block. A list's live entries come first and are distinct; direction 4 and directions leaving the grid hold only -1; some list holds 16 live entries. neighbours[e, f] is -1 (no coupling), a live slot of the same group, or 64 + d * 16 + k naming a live entry k of direction d of the sending group at offset -(dx, dy); slots at or beyond counts hold only -1.
All inputs are finite; a program needn't handle non-finite values.
Results may differ from a plain program's by a relative error of at most 0.0075.
The roundings to bfloat16 on the way count: a program that leaves them out, or rounds other values in their place, can miss the bound.
Values may be sent and summed in bfloat16 or wider, within the bound.
No kernel may reach another device: no remote copies, remote signals or barrier semaphores. Data moves between devices by JAX's collectives and lax.ppermute only.
A program may use at most 64 MiB of HBM per device.

v0:
```python
import jax
import jax.numpy as jnp
from jax import lax
from jax.sharding import PartitionSpec as P

POWERS = 4
HIGH = lax.Precision.HIGHEST


def passed_along(block, axis, distance):
    devices = range(lax.axis_size(axis))
    route = [(i - distance, i) for i in devices if i - distance in devices]
    return lax.ppermute(block, axis, route)


def forward_solve(factor, values):
    extent = factor.shape[-1]
    result = []
    for row_at in range(extent):
        running = values[:, row_at]
        for col_at in range(row_at):
            running = running - factor[:, row_at, col_at] * result[col_at]
        result.append(running / factor[:, row_at, row_at])
    return jnp.stack(result, axis=1)


def backward_solve(factor, values):
    extent = factor.shape[-1]
    result = [None] * extent
    for row_at in reversed(range(extent)):
        running = values[:, row_at]
        for col_at in range(row_at + 1, extent):
            running = running - factor[:, col_at, row_at] * result[col_at]
        result[row_at] = running / factor[:, row_at, row_at]
    return jnp.stack(result, axis=1)


def coefficients(gram):
    factor = jnp.linalg.cholesky(gram[:, 1:, 1:])
    return backward_solve(factor, forward_solve(factor, gram[:, 1:, 0]))


def fetch_ghosts(packets):
    empty = jnp.zeros_like(packets[4])
    columns = lax.axis_size("gy")
    column = lax.axis_index("gy")
    arrived = []
    for target in range(9):
        if target == 4:
            arrived.append(empty)
        else:
            step_row = target // 3 - 1
            step_col = target % 3 - 1
            shifted = passed_along(packets[target], ("gx", "gy"), step_row * columns + step_col)
            inside = (column - step_col >= 0) & (column - step_col < columns)
            arrived.append(jnp.where(inside, shifted, jnp.zeros((), jnp.bfloat16)))
    return jnp.stack(arrived)


def per_device(right_sides, diag_blocks, face_blocks, neighbours, send_slots, counts):
    capacity = right_sides.shape[0]
    slot_ids = lax.iota(jnp.int32, capacity)
    live_mask = (slot_ids < counts[0]).astype(jnp.float32)[:, None, None]
    outgoing = send_slots[0]
    sending = outgoing >= 0
    out_index = jnp.where(sending, outgoing, 0)
    present = neighbours >= 0
    source = jnp.where(present, neighbours, 0)
    zero_half = jnp.zeros((), jnp.bfloat16)
    vectors = [right_sides * live_mask]
    for step_index in range(POWERS):
        rounded = vectors[-1].astype(jnp.bfloat16)
        packets = jnp.where(sending[:, :, None, None], rounded[out_index], zero_half)
        ghosts = fetch_ghosts(packets)
        lookup = jnp.concatenate([rounded, ghosts.reshape((-1,) + rounded.shape[1:])], axis=0)
        gathered = jnp.where(present[:, :, None, None], lookup[source], zero_half)
        own_part = jnp.einsum(
            "eij,erj->eri", diag_blocks, rounded, preferred_element_type=jnp.float32
        )
        face_part = jnp.einsum(
            "efij,efrj->eri", face_blocks, gathered, preferred_element_type=jnp.float32
        )
        vectors.append((own_part + face_part) * live_mask)
    basis = jnp.stack(vectors)
    local_gram = jnp.einsum("icrn,jcrn->rij", basis, basis, precision=HIGH)
    gram = lax.psum(local_gram, ("gx", "gy"))
    weights = coefficients(gram)
    solution = jnp.einsum("rk,kcrn->crn", weights, basis[:POWERS], precision=HIGH)
    residual = basis[0] - jnp.einsum("rk,kcrn->crn", weights, basis[1:], precision=HIGH)
    return (solution, residual)


def solution(mesh):
    in_specs = (
        P(("gx", "gy"), None, None),
        P(("gx", "gy"), None, None),
        P(("gx", "gy"), None, None, None),
        P(("gx", "gy"), None),
        P(("gx", "gy"), None, None),
        P(("gx", "gy")),
    )
    out_specs = (P(("gx", "gy"), None, None), P(("gx", "gy"), None, None))
    return jax.shard_map(
        per_device, mesh=mesh, in_specs=in_specs, out_specs=out_specs, check_vma=False
    )
```

profile of v0, /device:TPU:1, one launch (start us, length us, event | category | flops | bytes accessed | tf_op | source)
XLA Modules:
  0.0 309.1 jit_solution(4113129172325548190)
XLA Ops:
  7.9 5.1 %collective-permute-start.1 = (bf16[16,8,128]{2,1,0:T(8,128)(2,1)}, bf16[16,8,128]{2,1,0:T(8,128)(2,1)}, u32[]{:S(2)}, u32[]{:S(2)}) collective-permute-start(bf16[16,8,128]{2,1,0:T(8,128)(2,1)} %get-tuple-element.53), channel_id=1, source_target_pairs={{16,0},{17,1},{18,2},{19,3},{20,4},{21,5},{22,6},{23,7},{24,8},{25... | collective-permute-start | bytes 98312 | tf_op jit(solution)/shard_map/ppermute | solution.py:13
  13.1 1.9 collective-permute-start.2
  15.0 6.2 %collective-permute-start.3 = (bf16[16,8,128]{2,1,0:T(8,128)(2,1)}, bf16[16,8,128]{2,1,0:T(8,128)(2,1)}, u32[]{:S(2)}, u32[]{:S(2)}) collective-permute-start(bf16[16,8,128]{2,1,0:T(8,128)(2,1)} %get-tuple-element.51), channel_id=1, source_target_pairs={{1,0},{2,1},{3,2},{4,3},{5,4},{6,5},{7,6},{8,7},{9,8},{10,9},{11,1... | collective-permute-start | bytes 98312 | tf_op jit(solution)/shard_map/ppermute | solution.py:13
  21.2 1.9 collective-permute-start.4
  23.2 1.8 constant_dynamic-update-slice_fusion.40
  26.2 8.3 %collective-permute-start.5 = (bf16[16,8,128]{2,1,0:T(8,128)(2,1)}, bf16[16,8,128]{2,1,0:T(8,128)(2,1)S(1)}, u32[]{:S(2)}, u32[]{:S(2)}) collective-permute-start(bf16[16,8,128]{2,1,0:T(8,128)(2,1)} %get-tuple-element.49), channel_id=1, source_target_pairs={{0,15},{1,16},{2,17},{3,18},{4,19},{5,20},{6,21},{7,22},{8,23},{9,... | collective-permute-start | bytes 98312 | tf_op jit(solution)/shard_map/ppermute | solution.py:13
  35.3 6.7 %collective-permute-start.6 = (bf16[16,8,128]{2,1,0:T(8,128)(2,1)}, bf16[16,8,128]{2,1,0:T(8,128)(2,1)S(1)}, u32[]{:S(2)}, u32[]{:S(2)}) collective-permute-start(bf16[16,8,128]{2,1,0:T(8,128)(2,1)} %get-tuple-element.48), channel_id=1, source_target_pairs={{0,16},{1,17},{2,18},{3,19},{4,20},{5,21},{6,22},{7,23},{8,24},{9,... | collective-permute-start | bytes 98312 | tf_op jit(solution)/shard_map/ppermute | solution.py:13
  46.3 2.6 gather_fusion.1
  48.9 5.9 %convolution_bitcast_fusion.3 = f32[64,8,128]{2,1,0:T(8,128)S(1)} fusion(bf16[64,4,128,128]{3,2,1,0:T(8,128)(2,1)} %param.8, bf16[64,4,8,128]{3,2,1,0:T(8,128)(2,1)} %bitcast.295, pred[64,4]{1,0:T(8,128)(4,1)S(1)} %copy.36), kind=kOutput, calls=%fused_computation.20 | convolution fusion | flops 67371008 | bytes 9175296 | tf_op jit(solution)/shard_map/efij,efrj->eri/dot_general | solution.py:80
  56.7 1.4 gather_fusion.2
  59.4 1.3 collective-permute-start.8
  60.7 1.9 collective-permute-start.9
  62.6 1.9 collective-permute-start.10
  64.5 8.1 %collective-permute-start.11 = (bf16[16,8,128]{2,1,0:T(8,128)(2,1)S(1)}, bf16[16,8,128]{2,1,0:T(8,128)(2,1)S(1)}, u32[]{:S(2)}, u32[]{:S(2)}) collective-permute-start(bf16[16,8,128]{2,1,0:T(8,128)(2,1)S(1)} %get-tuple-element.43), channel_id=1, source_target_pairs={{1,0},{2,1},{3,2},{4,3},{5,4},{6,5},{7,6},{8,7},{9,8},{10,9},{11,1... | collective-permute-start | bytes 98312 | tf_op jit(solution)/shard_map/ppermute | solution.py:13
  72.6 1.9 collective-permute-start.12
  74.5 9.5 %collective-permute-start.13 = (bf16[16,8,128]{2,1,0:T(8,128)(2,1)S(1)}, bf16[16,8,128]{2,1,0:T(8,128)(2,1)S(1)}, u32[]{:S(2)}, u32[]{:S(2)}) collective-permute-start(bf16[16,8,128]{2,1,0:T(8,128)(2,1)S(1)} %get-tuple-element.41), channel_id=1, source_target_pairs={{0,15},{1,16},{2,17},{3,18},{4,19},{5,20},{6,21},{7,22},{8,23},{9,... | collective-permute-start | bytes 98312 | tf_op jit(solution)/shard_map/ppermute | solution.py:13
  84.1 7.8 %collective-permute-start.14 = (bf16[16,8,128]{2,1,0:T(8,128)(2,1)S(1)}, bf16[16,8,128]{2,1,0:T(8,128)(2,1)S(1)}, u32[]{:S(2)}, u32[]{:S(2)}) collective-permute-start(bf16[16,8,128]{2,1,0:T(8,128)(2,1)S(1)} %get-tuple-element.40), channel_id=1, source_target_pairs={{0,16},{1,17},{2,18},{3,19},{4,20},{5,21},{6,22},{7,23},{8,24},{9,... | collective-permute-start | bytes 98312 | tf_op jit(solution)/shard_map/ppermute | solution.py:13
  91.9 1.3 collective-permute-start.15
  95.0 2.6 gather_fusion.3
  97.6 5.9 %convolution_bitcast_fusion.2 = f32[64,8,128]{2,1,0:T(8,128)S(1)} fusion(bf16[64,4,128,128]{3,2,1,0:T(8,128)(2,1)} %param.8, bf16[64,4,8,128]{3,2,1,0:T(8,128)(2,1)} %bitcast.296, pred[64,4]{1,0:T(8,128)(4,1)S(1)} %copy.36), kind=kOutput, calls=%fused_computation.17 | convolution fusion | flops 67371008 | bytes 9175296 | tf_op jit(solution)/shard_map/efij,efrj->eri/dot_general | solution.py:80
  105.4 1.4 gather_fusion.4
  108.0 1.3 collective-permute-start.16
  109.8 1.9 collective-permute-start.17
  111.8 1.9 collective-permute-start.18
  113.7 8.1 %collective-permute-start.19 = (bf16[16,8,128]{2,1,0:T(8,128)(2,1)S(1)}, bf16[16,8,128]{2,1,0:T(8,128)(2,1)S(1)}, u32[]{:S(2)}, u32[]{:S(2)}) collective-permute-start(bf16[16,8,128]{2,1,0:T(8,128)(2,1)S(1)} %get-tuple-element.35), channel_id=1, source_target_pairs={{1,0},{2,1},{3,2},{4,3},{5,4},{6,5},{7,6},{8,7},{9,8},{10,9},{11,1... | collective-permute-start | bytes 98312 | tf_op jit(solution)/shard_map/ppermute | solution.py:13
  121.8 1.9 collective-permute-start.20
  123.7 9.5 %collective-permute-start.21 = (bf16[16,8,128]{2,1,0:T(8,128)(2,1)S(1)}, bf16[16,8,128]{2,1,0:T(8,128)(2,1)S(1)}, u32[]{:S(2)}, u32[]{:S(2)}) collective-permute-start(bf16[16,8,128]{2,1,0:T(8,128)(2,1)S(1)} %get-tuple-element.33), channel_id=1, source_target_pairs={{0,15},{1,16},{2,17},{3,18},{4,19},{5,20},{6,21},{7,22},{8,23},{9,... | collective-permute-start | bytes 98312 | tf_op jit(solution)/shard_map/ppermute | solution.py:13
  133.3 7.8 %collective-permute-start.22 = (bf16[16,8,128]{2,1,0:T(8,128)(2,1)S(1)}, bf16[16,8,128]{2,1,0:T(8,128)(2,1)S(1)}, u32[]{:S(2)}, u32[]{:S(2)}) collective-permute-start(bf16[16,8,128]{2,1,0:T(8,128)(2,1)S(1)} %get-tuple-element.32), channel_id=1, source_target_pairs={{0,16},{1,17},{2,18},{3,19},{4,20},{5,21},{6,22},{7,23},{8,24},{9,... | collective-permute-start | bytes 98312 | tf_op jit(solution)/shard_map/ppermute | solution.py:13
  144.3 2.6 gather_fusion.5
  146.9 5.9 %convolution_bitcast_fusion.1 = f32[64,8,128]{2,1,0:T(8,128)S(1)} fusion(bf16[64,4,128,128]{3,2,1,0:T(8,128)(2,1)} %param.8, bf16[64,4,8,128]{3,2,1,0:T(8,128)(2,1)} %bitcast.297, pred[64,4]{1,0:T(8,128)(4,1)S(1)} %copy.36), kind=kOutput, calls=%fused_computation.14 | convolution fusion | flops 67371008 | bytes 9175296 | tf_op jit(solution)/shard_map/efij,efrj->eri/dot_general | solution.py:80
  154.7 1.4 gather_fusion.6
  157.3 1.3 collective-permute-start.24
  159.1 1.9 collective-permute-start.25
  161.0 1.9 collective-permute-start.26
  162.9 8.2 %collective-permute-start.27 = (bf16[16,8,128]{2,1,0:T(8,128)(2,1)S(1)}, bf16[16,8,128]{2,1,0:T(8,128)(2,1)S(1)}, u32[]{:S(2)}, u32[]{:S(2)}) collective-permute-start(bf16[16,8,128]{2,1,0:T(8,128)(2,1)S(1)} %get-tuple-element.27), channel_id=1, source_target_pairs={{1,0},{2,1},{3,2},{4,3},{5,4},{6,5},{7,6},{8,7},{9,8},{10,9},{11,1... | collective-permute-start | bytes 98312 | tf_op jit(solution)/shard_map/ppermute | solution.py:13
  171.1 1.9 collective-permute-start.28
  173.0 9.6 %collective-permute-start.29 = (bf16[16,8,128]{2,1,0:T(8,128)(2,1)S(1)}, bf16[16,8,128]{2,1,0:T(8,128)(2,1)S(1)}, u32[]{:S(2)}, u32[]{:S(2)}) collective-permute-start(bf16[16,8,128]{2,1,0:T(8,128)(2,1)S(1)} %get-tuple-element.25), channel_id=1, source_target_pairs={{0,15},{1,16},{2,17},{3,18},{4,19},{5,20},{6,21},{7,22},{8,23},{9,... | collective-permute-start | bytes 98312 | tf_op jit(solution)/shard_map/ppermute | solution.py:13
  182.7 7.8 %collective-permute-start.30 = (bf16[16,8,128]{2,1,0:T(8,128)(2,1)S(1)}, bf16[16,8,128]{2,1,0:T(8,128)(2,1)S(1)}, u32[]{:S(2)}, u32[]{:S(2)}) collective-permute-start(bf16[16,8,128]{2,1,0:T(8,128)(2,1)S(1)} %get-tuple-element.24), channel_id=1, source_target_pairs={{0,16},{1,17},{2,18},{3,19},{4,20},{5,21},{6,22},{7,23},{8,24},{9,... | collective-permute-start | bytes 98312 | tf_op jit(solution)/shard_map/ppermute | solution.py:13
  190.5 1.5 collective-permute-start.31
  193.6 2.6 gather_fusion.7
  196.2 5.9 %convolution_bitcast_fusion = f32[64,8,128]{2,1,0:T(8,128)S(1)} fusion(bf16[64,4,128,128]{3,2,1,0:T(8,128)(2,1)} %param.8, bf16[64,4,8,128]{3,2,1,0:T(8,128)(2,1)} %bitcast.294, pred[64,4]{1,0:T(8,128)(4,1)S(1)} %copy.36), kind=kOutput, calls=%fused_computation.10 | convolution fusion | flops 67371008 | bytes 9175296 | tf_op jit(solution)/shard_map/efij,efrj->eri/dot_general | solution.py:80
  202.1 1.9 constant_dynamic-update-slice_fusion.36
  204.0 4.9 %fusion.7 = f32[8,5,5]{1,2,0:T(8,128)S(1)} fusion(f32[5,64,8,128]{3,2,1,0:T(8,128)S(1)} %get-tuple-element.61), kind=kOutput, calls=%fused_computation.23 | convolution fusion | flops 19660800 | bytes 1311520 | tf_op jit(solution)/shard_map/icrn,jcrn->rij/dot_general | solution.py:85
  209.0 87.5 %psum.7 = f32[8,5,5]{1,2,0:T(8,128)S(1)} all-reduce(f32[8,5,5]{1,2,0:T(8,128)S(1)} %fusion.7), channel_id=1, replica_groups=mesh['gx'=16,'gy'=16] {'gx','gy'}, use_global_device_ids=true, to_apply=%region_0.1 | all-reduce | flops 200 | bytes 1600 | tf_op jit(solution)/shard_map/psum | solution.py:86
  296.9 3.0 custom-call.4
  300.6 1.7 pad_maximum_fusion.1
  302.3 2.5 fusion.12
  305.7 2.5 fusion.10
  (148 shorter events, 32.5 us)
Async XLA Ops:
  0.6 54.1 %copy-start = (bf16[64,128,128]{2,1,0:T(8,128)(2,1)S(1)}, bf16[64,128,128]{2,1,0:T(8,128)(2,1)}, u32[]{:S(2)}) copy-start(bf16[64,128,128]{2,1,0:T(8,128)(2,1)} %param.7) | copy-start | bytes 6291460
  0.6 24.3 %copy-start.11 = (s32[64,4]{0,1:T(4,128)S(1)}, s32[64,4]{0,1:T(4,128)}, u32[]{:S(2)}) copy-start(s32[64,4]{0,1:T(4,128)} %param.9) | copy-start | bytes 3076
  2.9 22.6 %copy-start.6 = (f32[64]{0:T(128)}, f32[64]{0:T(128)S(1)}, u32[]{:S(2)}) copy-start(f32[64]{0:T(128)S(1)} %compare_convert_fusion) | copy-start | bytes 772
  3.9 17.3 %copy-start.5 = (pred[1,9,16]{2,1,0:T(8,128)(4,1)}, pred[1,9,16]{2,1,0:T(8,128)(4,1)S(1)}, u32[]{:S(2)}) copy-start(pred[1,9,16]{2,1,0:T(8,128)(4,1)S(1)} %copy.69) | copy-start | bytes 436
  6.6 19.6 %collective-permute-start = (bf16[16,8,128]{2,1,0:T(8,128)(2,1)}, bf16[16,8,128]{2,1,0:T(8,128)(2,1)}, u32[]{:S(2)}, u32[]{:S(2)}) collective-permute-start(bf16[16,8,128]{2,1,0:T(8,128)(2,1)} %get-tuple-element.54), channel_id=1, source_target_pairs={{17,0},{18,1},{19,2},{20,3},{21,4},{22,5},{23,6},{24,7},{25,8},{26... | collective-permute-start | bytes 98312 | tf_op jit(solution)/shard_map/ppermute | solution.py:13
  7.9 27.4 %collective-permute-start.1 = (bf16[16,8,128]{2,1,0:T(8,128)(2,1)}, bf16[16,8,128]{2,1,0:T(8,128)(2,1)}, u32[]{:S(2)}, u32[]{:S(2)}) collective-permute-start(bf16[16,8,128]{2,1,0:T(8,128)(2,1)} %get-tuple-element.53), channel_id=1, source_target_pairs={{16,0},{17,1},{18,2},{19,3},{20,4},{21,5},{22,6},{23,7},{24,8},{25... | collective-permute-start | bytes 98312 | tf_op jit(solution)/shard_map/ppermute | solution.py:13
  13.1 29.8 %collective-permute-start.2 = (bf16[16,8,128]{2,1,0:T(8,128)(2,1)}, bf16[16,8,128]{2,1,0:T(8,128)(2,1)}, u32[]{:S(2)}, u32[]{:S(2)}) collective-permute-start(bf16[16,8,128]{2,1,0:T(8,128)(2,1)} %get-tuple-element.52), channel_id=1, source_target_pairs={{15,0},{16,1},{17,2},{18,3},{19,4},{20,5},{21,6},{22,7},{23,8},{24... | collective-permute-start | bytes 98312 | tf_op jit(solution)/shard_map/ppermute | solution.py:13
  15.0 29.2 %collective-permute-start.3 = (bf16[16,8,128]{2,1,0:T(8,128)(2,1)}, bf16[16,8,128]{2,1,0:T(8,128)(2,1)}, u32[]{:S(2)}, u32[]{:S(2)}) collective-permute-start(bf16[16,8,128]{2,1,0:T(8,128)(2,1)} %get-tuple-element.51), channel_id=1, source_target_pairs={{1,0},{2,1},{3,2},{4,3},{5,4},{6,5},{7,6},{8,7},{9,8},{10,9},{11,1... | collective-permute-start | bytes 98312 | tf_op jit(solution)/shard_map/ppermute | solution.py:13
  21.2 23.8 %collective-permute-start.4 = (bf16[16,8,128]{2,1,0:T(8,128)(2,1)}, bf16[16,8,128]{2,1,0:T(8,128)(2,1)}, u32[]{:S(2)}, u32[]{:S(2)}) collective-permute-start(bf16[16,8,128]{2,1,0:T(8,128)(2,1)} %get-tuple-element.50), channel_id=1, source_target_pairs={{0,1},{1,2},{2,3},{3,4},{4,5},{5,6},{6,7},{7,8},{8,9},{9,10},{10,1... | collective-permute-start | bytes 98312 | tf_op jit(solution)/shard_map/ppermute | solution.py:13
  26.2 18.8 %collective-permute-start.5 = (bf16[16,8,128]{2,1,0:T(8,128)(2,1)}, bf16[16,8,128]{2,1,0:T(8,128)(2,1)S(1)}, u32[]{:S(2)}, u32[]{:S(2)}) collective-permute-start(bf16[16,8,128]{2,1,0:T(8,128)(2,1)} %get-tuple-element.49), channel_id=1, source_target_pairs={{0,15},{1,16},{2,17},{3,18},{4,19},{5,20},{6,21},{7,22},{8,23},{9,... | collective-permute-start | bytes 98312 | tf_op jit(solution)/shard_map/ppermute | solution.py:13
  35.3 9.8 %collective-permute-start.6 = (bf16[16,8,128]{2,1,0:T(8,128)(2,1)}, bf16[16,8,128]{2,1,0:T(8,128)(2,1)S(1)}, u32[]{:S(2)}, u32[]{:S(2)}) collective-permute-start(bf16[16,8,128]{2,1,0:T(8,128)(2,1)} %get-tuple-element.48), channel_id=1, source_target_pairs={{0,16},{1,17},{2,18},{3,19},{4,20},{5,21},{6,22},{7,23},{8,24},{9,... | collective-permute-start | bytes 98312 | tf_op jit(solution)/shard_map/ppermute | solution.py:13
  42.9 2.6 collective-permute-start.7
  48.9 5.9 %copy-start.7 = (f32[64]{0:T(128)S(1)}, f32[64]{0:T(128)}, u32[]{:S(2)}) copy-start(f32[64]{0:T(128)} %copy-done.6) | copy-start | bytes 772
  56.0 0.7 copy-start.2
  59.4 15.2 %collective-permute-start.8 = (bf16[16,8,128]{2,1,0:T(8,128)(2,1)S(1)}, bf16[16,8,128]{2,1,0:T(8,128)(2,1)S(1)}, u32[]{:S(2)}, u32[]{:S(2)}) collective-permute-start(bf16[16,8,128]{2,1,0:T(8,128)(2,1)S(1)} %get-tuple-element.46), channel_id=1, source_target_pairs={{17,0},{18,1},{19,2},{20,3},{21,4},{22,5},{23,6},{24,7},{25,8},{26... | collective-permute-start | bytes 98312 | tf_op jit(solution)/shard_map/ppermute | solution.py:13
  60.7 23.4 %collective-permute-start.9 = (bf16[16,8,128]{2,1,0:T(8,128)(2,1)S(1)}, bf16[16,8,128]{2,1,0:T(8,128)(2,1)S(1)}, u32[]{:S(2)}, u32[]{:S(2)}) collective-permute-start(bf16[16,8,128]{2,1,0:T(8,128)(2,1)S(1)} %get-tuple-element.45), channel_id=1, source_target_pairs={{16,0},{17,1},{18,2},{19,3},{20,4},{21,5},{22,6},{23,7},{24,8},{25... | collective-permute-start | bytes 98312 | tf_op jit(solution)/shard_map/ppermute | solution.py:13
  62.6 29.3 %collective-permute-start.10 = (bf16[16,8,128]{2,1,0:T(8,128)(2,1)S(1)}, bf16[16,8,128]{2,1,0:T(8,128)(2,1)S(1)}, u32[]{:S(2)}, u32[]{:S(2)}) collective-permute-start(bf16[16,8,128]{2,1,0:T(8,128)(2,1)S(1)} %get-tuple-element.44), channel_id=1, source_target_pairs={{15,0},{16,1},{17,2},{18,3},{19,4},{20,5},{21,6},{22,7},{23,8},{24... | collective-permute-start | bytes 98312 | tf_op jit(solution)/shard_map/ppermute | solution.py:13
  64.5 28.7 %collective-permute-start.11 = (bf16[16,8,128]{2,1,0:T(8,128)(2,1)S(1)}, bf16[16,8,128]{2,1,0:T(8,128)(2,1)S(1)}, u32[]{:S(2)}, u32[]{:S(2)}) collective-permute-start(bf16[16,8,128]{2,1,0:T(8,128)(2,1)S(1)} %get-tuple-element.43), channel_id=1, source_target_pairs={{1,0},{2,1},{3,2},{4,3},{5,4},{6,5},{7,6},{8,7},{9,8},{10,9},{11,1... | collective-permute-start | bytes 98312 | tf_op jit(solution)/shard_map/ppermute | solution.py:13
  72.6 20.6 %collective-permute-start.12 = (bf16[16,8,128]{2,1,0:T(8,128)(2,1)S(1)}, bf16[16,8,128]{2,1,0:T(8,128)(2,1)S(1)}, u32[]{:S(2)}, u32[]{:S(2)}) collective-permute-start(bf16[16,8,128]{2,1,0:T(8,128)(2,1)S(1)} %get-tuple-element.42), channel_id=1, source_target_pairs={{0,1},{1,2},{2,3},{3,4},{4,5},{5,6},{6,7},{7,8},{8,9},{9,10},{10,1... | collective-permute-start | bytes 98312 | tf_op jit(solution)/shard_map/ppermute | solution.py:13
  74.5 18.7 %collective-permute-start.13 = (bf16[16,8,128]{2,1,0:T(8,128)(2,1)S(1)}, bf16[16,8,128]{2,1,0:T(8,128)(2,1)S(1)}, u32[]{:S(2)}, u32[]{:S(2)}) collective-permute-start(bf16[16,8,128]{2,1,0:T(8,128)(2,1)S(1)} %get-tuple-element.41), channel_id=1, source_target_pairs={{0,15},{1,16},{2,17},{3,18},{4,19},{5,20},{6,21},{7,22},{8,23},{9,... | collective-permute-start | bytes 98312 | tf_op jit(solution)/shard_map/ppermute | solution.py:13
  84.1 9.2 %collective-permute-start.14 = (bf16[16,8,128]{2,1,0:T(8,128)(2,1)S(1)}, bf16[16,8,128]{2,1,0:T(8,128)(2,1)S(1)}, u32[]{:S(2)}, u32[]{:S(2)}) collective-permute-start(bf16[16,8,128]{2,1,0:T(8,128)(2,1)S(1)} %get-tuple-element.40), channel_id=1, source_target_pairs={{0,16},{1,17},{2,18},{3,19},{4,20},{5,21},{6,22},{7,23},{8,24},{9,... | collective-permute-start | bytes 98312 | tf_op jit(solution)/shard_map/ppermute | solution.py:13
  91.9 2.3 collective-permute-start.15
  97.6 5.9 %copy-start.8 = (f32[64]{0:T(128)S(1)}, f32[64]{0:T(128)}, u32[]{:S(2)}) copy-start(f32[64]{0:T(128)} %copy-done.6) | copy-start | bytes 772
  104.7 0.7 copy-start.3
  108.0 15.7 %collective-permute-start.16 = (bf16[16,8,128]{2,1,0:T(8,128)(2,1)S(1)}, bf16[16,8,128]{2,1,0:T(8,128)(2,1)S(1)}, u32[]{:S(2)}, u32[]{:S(2)}) collective-permute-start(bf16[16,8,128]{2,1,0:T(8,128)(2,1)S(1)} %get-tuple-element.38), channel_id=1, source_target_pairs={{17,0},{18,1},{19,2},{20,3},{21,4},{22,5},{23,6},{24,7},{25,8},{26... | collective-permute-start | bytes 98312 | tf_op jit(solution)/shard_map/ppermute | solution.py:13
  109.8 23.4 %collective-permute-start.17 = (bf16[16,8,128]{2,1,0:T(8,128)(2,1)S(1)}, bf16[16,8,128]{2,1,0:T(8,128)(2,1)S(1)}, u32[]{:S(2)}, u32[]{:S(2)}) collective-permute-start(bf16[16,8,128]{2,1,0:T(8,128)(2,1)S(1)} %get-tuple-element.37), channel_id=1, source_target_pairs={{16,0},{17,1},{18,2},{19,3},{20,4},{21,5},{22,6},{23,7},{24,8},{25... | collective-permute-start | bytes 98312 | tf_op jit(solution)/shard_map/ppermute | solution.py:13
  111.8 29.4 %collective-permute-start.18 = (bf16[16,8,128]{2,1,0:T(8,128)(2,1)S(1)}, bf16[16,8,128]{2,1,0:T(8,128)(2,1)S(1)}, u32[]{:S(2)}, u32[]{:S(2)}) collective-permute-start(bf16[16,8,128]{2,1,0:T(8,128)(2,1)S(1)} %get-tuple-element.36), channel_id=1, source_target_pairs={{15,0},{16,1},{17,2},{18,3},{19,4},{20,5},{21,6},{22,7},{23,8},{24... | collective-permute-start | bytes 98312 | tf_op jit(solution)/shard_map/ppermute | solution.py:13
  113.7 28.8 %collective-permute-start.19 = (bf16[16,8,128]{2,1,0:T(8,128)(2,1)S(1)}, bf16[16,8,128]{2,1,0:T(8,128)(2,1)S(1)}, u32[]{:S(2)}, u32[]{:S(2)}) collective-permute-start(bf16[16,8,128]{2,1,0:T(8,128)(2,1)S(1)} %get-tuple-element.35), channel_id=1, source_target_pairs={{1,0},{2,1},{3,2},{4,3},{5,4},{6,5},{7,6},{8,7},{9,8},{10,9},{11,1... | collective-permute-start | bytes 98312 | tf_op jit(solution)/shard_map/ppermute | solution.py:13
  121.8 20.7 %collective-permute-start.20 = (bf16[16,8,128]{2,1,0:T(8,128)(2,1)S(1)}, bf16[16,8,128]{2,1,0:T(8,128)(2,1)S(1)}, u32[]{:S(2)}, u32[]{:S(2)}) collective-permute-start(bf16[16,8,128]{2,1,0:T(8,128)(2,1)S(1)} %get-tuple-element.34), channel_id=1, source_target_pairs={{0,1},{1,2},{2,3},{3,4},{4,5},{5,6},{6,7},{7,8},{8,9},{9,10},{10,1... | collective-permute-start | bytes 98312 | tf_op jit(solution)/shard_map/ppermute | solution.py:13
  123.7 18.8 %collective-permute-start.21 = (bf16[16,8,128]{2,1,0:T(8,128)(2,1)S(1)}, bf16[16,8,128]{2,1,0:T(8,128)(2,1)S(1)}, u32[]{:S(2)}, u32[]{:S(2)}) collective-permute-start(bf16[16,8,128]{2,1,0:T(8,128)(2,1)S(1)} %get-tuple-element.33), channel_id=1, source_target_pairs={{0,15},{1,16},{2,17},{3,18},{4,19},{5,20},{6,21},{7,22},{8,23},{9,... | collective-permute-start | bytes 98312 | tf_op jit(solution)/shard_map/ppermute | solution.py:13
  133.3 9.3 %collective-permute-start.22 = (bf16[16,8,128]{2,1,0:T(8,128)(2,1)S(1)}, bf16[16,8,128]{2,1,0:T(8,128)(2,1)S(1)}, u32[]{:S(2)}, u32[]{:S(2)}) collective-permute-start(bf16[16,8,128]{2,1,0:T(8,128)(2,1)S(1)} %get-tuple-element.32), channel_id=1, source_target_pairs={{0,16},{1,17},{2,18},{3,19},{4,20},{5,21},{6,22},{7,23},{8,24},{9,... | collective-permute-start | bytes 98312 | tf_op jit(solution)/shard_map/ppermute | solution.py:13
  141.1 2.3 collective-permute-start.23
  146.9 5.9 %copy-start.9 = (f32[64]{0:T(128)S(1)}, f32[64]{0:T(128)}, u32[]{:S(2)}) copy-start(f32[64]{0:T(128)} %copy-done.6) | copy-start | bytes 772
  153.9 0.7 copy-start.4
  157.3 15.7 %collective-permute-start.24 = (bf16[16,8,128]{2,1,0:T(8,128)(2,1)S(1)}, bf16[16,8,128]{2,1,0:T(8,128)(2,1)S(1)}, u32[]{:S(2)}, u32[]{:S(2)}) collective-permute-start(bf16[16,8,128]{2,1,0:T(8,128)(2,1)S(1)} %get-tuple-element.30), channel_id=1, source_target_pairs={{17,0},{18,1},{19,2},{20,3},{21,4},{22,5},{23,6},{24,7},{25,8},{26... | collective-permute-start | bytes 98312 | tf_op jit(solution)/shard_map/ppermute | solution.py:13
  159.1 23.6 %collective-permute-start.25 = (bf16[16,8,128]{2,1,0:T(8,128)(2,1)S(1)}, bf16[16,8,128]{2,1,0:T(8,128)(2,1)S(1)}, u32[]{:S(2)}, u32[]{:S(2)}) collective-permute-start(bf16[16,8,128]{2,1,0:T(8,128)(2,1)S(1)} %get-tuple-element.29), channel_id=1, source_target_pairs={{16,0},{17,1},{18,2},{19,3},{20,4},{21,5},{22,6},{23,7},{24,8},{25... | collective-permute-start | bytes 98312 | tf_op jit(solution)/shard_map/ppermute | solution.py:13
  161.0 29.5 %collective-permute-start.26 = (bf16[16,8,128]{2,1,0:T(8,128)(2,1)S(1)}, bf16[16,8,128]{2,1,0:T(8,128)(2,1)S(1)}, u32[]{:S(2)}, u32[]{:S(2)}) collective-permute-start(bf16[16,8,128]{2,1,0:T(8,128)(2,1)S(1)} %get-tuple-element.28), channel_id=1, source_target_pairs={{15,0},{16,1},{17,2},{18,3},{19,4},{20,5},{21,6},{22,7},{23,8},{24... | collective-permute-start | bytes 98312 | tf_op jit(solution)/shard_map/ppermute | solution.py:13
  162.9 29.1 %collective-permute-start.27 = (bf16[16,8,128]{2,1,0:T(8,128)(2,1)S(1)}, bf16[16,8,128]{2,1,0:T(8,128)(2,1)S(1)}, u32[]{:S(2)}, u32[]{:S(2)}) collective-permute-start(bf16[16,8,128]{2,1,0:T(8,128)(2,1)S(1)} %get-tuple-element.27), channel_id=1, source_target_pairs={{1,0},{2,1},{3,2},{4,3},{5,4},{6,5},{7,6},{8,7},{9,8},{10,9},{11,1... | collective-permute-start | bytes 98312 | tf_op jit(solution)/shard_map/ppermute | solution.py:13
  171.1 21.0 %collective-permute-start.28 = (bf16[16,8,128]{2,1,0:T(8,128)(2,1)S(1)}, bf16[16,8,128]{2,1,0:T(8,128)(2,1)S(1)}, u32[]{:S(2)}, u32[]{:S(2)}) collective-permute-start(bf16[16,8,128]{2,1,0:T(8,128)(2,1)S(1)} %get-tuple-element.26), channel_id=1, source_target_pairs={{0,1},{1,2},{2,3},{3,4},{4,5},{5,6},{6,7},{7,8},{8,9},{9,10},{10,1... | collective-permute-start | bytes 98312 | tf_op jit(solution)/shard_map/ppermute | solution.py:13
  173.0 19.0 %collective-permute-start.29 = (bf16[16,8,128]{2,1,0:T(8,128)(2,1)S(1)}, bf16[16,8,128]{2,1,0:T(8,128)(2,1)S(1)}, u32[]{:S(2)}, u32[]{:S(2)}) collective-permute-start(bf16[16,8,128]{2,1,0:T(8,128)(2,1)S(1)} %get-tuple-element.25), channel_id=1, source_target_pairs={{0,15},{1,16},{2,17},{3,18},{4,19},{5,20},{6,21},{7,22},{8,23},{9,... | collective-permute-start | bytes 98312 | tf_op jit(solution)/shard_map/ppermute | solution.py:13
  182.7 9.5 %collective-permute-start.30 = (bf16[16,8,128]{2,1,0:T(8,128)(2,1)S(1)}, bf16[16,8,128]{2,1,0:T(8,128)(2,1)S(1)}, u32[]{:S(2)}, u32[]{:S(2)}) collective-permute-start(bf16[16,8,128]{2,1,0:T(8,128)(2,1)S(1)} %get-tuple-element.24), channel_id=1, source_target_pairs={{0,16},{1,17},{2,18},{3,19},{4,20},{5,21},{6,22},{7,23},{8,24},{9,... | collective-permute-start | bytes 98312 | tf_op jit(solution)/shard_map/ppermute | solution.py:13
  190.5 2.3 collective-permute-start.31
  196.2 5.9 %copy-start.10 = (f32[64]{0:T(128)S(1)}, f32[64]{0:T(128)}, u32[]{:S(2)}) copy-start(f32[64]{0:T(128)} %copy-done.6) | copy-start | bytes 772
  204.0 95.9 %copy-start.13 = (pred[4,4]{1,0:T(4,128)(4,1)S(1)}, pred[4,4]{1,0:T(4,128)(4,1)}, u32[]{:S(2)}) copy-start(pred[4,4]{1,0:T(4,128)(4,1)} %iota_compare_fusion) | copy-start | bytes 52
  204.0 96.0 %copy-start.12 = (pred[4,4]{1,0:T(4,128)(4,1)S(1)}, pred[4,4]{1,0:T(4,128)(4,1)}, u32[]{:S(2)}) copy-start(pred[4,4]{1,0:T(4,128)(4,1)} %iota_compare_fusion.1) | copy-start | bytes 52
  302.3 5.9 %copy-start.1 = (f32[64,8,128]{2,1,0:T(8,128)S(1)}, f32[64,8,128]{2,1,0:T(8,128)}, u32[]{:S(2)}) copy-start(f32[64,8,128]{2,1,0:T(8,128)} %param.6) | copy-start | bytes 786436
where the time goes:
time: 311 us; the launch traced here: 309 us
  starting transfers between devices  134 us (43%)
  blocking collectives  87.5 us (28%)
  matrix products  38.9 us (13%)
  other arithmetic  22.7 us (7%)
  local copies, waits for them, and re-layouts  20.8 us (7%)
    ppermute x32, starting transfers between devices, passed_along(): return lax.ppermute(block, axis, route)  134 us
    psum x1, blocking collectives, per_device(): gram = lax.psum(local_gram, ('gx', 'gy'))  87.5 us
    dot_general x4, matrix products, per_device(): jnp.einsum('efij,efrj->eri', face_blocks, gathered, preferred_element_typ...  23.5 us
    gather x4, local copies, waits for them, and re-layouts, per_device(): gathered = jnp.where(present[:, :, None, None], lookup[source], zero_half)  10.4 us
  transfers between devices with their start and end apart: 32, of which 4 were waited for; matrix products, arithmetic and copies ran while one was open for 2% of the time, Pallas kernels for 0%

commit v1 on v0

--- a/solution.py
+++ b/solution.py
@@ -83,7 +83,7 @@
         vectors.append((own_part + face_part) * live_mask)
     basis = jnp.stack(vectors)
     local_gram = jnp.einsum("icrn,jcrn->rij", basis, basis, precision=HIGH)
-    gram = lax.psum(local_gram, ("gx", "gy"))
+    gram = lax.psum(lax.psum(local_gram, "gx"), "gy")
     weights = coefficients(gram)
     solution = jnp.einsum("rk,kcrn->crn", weights, basis[:POWERS], precision=HIGH)
     residual = basis[0] - jnp.einsum("rk,kcrn->crn", weights, basis[1:], precision=HIGH)

time: 311 us -> 350 us (1.13)
  the two profiles are of different devices: /device:TPU:1 before, /device:TPU:128 now
where the time goes in v1:
time: 350 us; the launch traced here: 348 us
  blocking collectives  116 us (33%)
  starting transfers between devices  111 us (32%)
  matrix products  38.9 us (11%)
  waiting for transfers between devices  36.9 us (11%)
  other arithmetic  22.7 us (6%)
  local copies, waits for them, and re-layouts  20.6 us (6%)
    psum x2, blocking collectives, per_device(): gram = lax.psum(lax.psum(local_gram, 'gx'), 'gy')  116 us
    ppermute x32, starting transfers between devices, passed_along(): return lax.ppermute(block, axis, route)  111 us
    ppermute x32, waiting for transfers between devices, passed_along(): return lax.ppermute(block, axis, route)  36.9 us
    dot_general x4, matrix products, per_device(): jnp.einsum('efij,efrj->eri', face_blocks, gathered, preferred_element_typ...  23.5 us
    gather x4, local copies, waits for them, and re-layouts, per_device(): gathered = jnp.where(present[:, :, None, None], lookup[source], zero_half)  10.3 us
  transfers between devices with their start and end apart: 32, of which 8 were waited for; matrix products, arithmetic and copies ran while one was open for 2% of the time, Pallas kernels for 0%

profile of v1, /device:TPU:128, one launch (start us, length us, event | category | flops | bytes accessed | tf_op | source)
XLA Modules:
  0.0 347.8 jit_solution(17466798394831512470)
XLA Ops:
  6.6 6.7 %collective-permute-start = (bf16[16,8,128]{2,1,0:T(8,128)(2,1)}, bf16[16,8,128]{2,1,0:T(8,128)(2,1)}, u32[]{:S(2)}, u32[]{:S(2)}) collective-permute-start(bf16[16,8,128]{2,1,0:T(8,128)(2,1)} %get-tuple-element.54), channel_id=1, source_target_pairs={{17,0},{18,1},{19,2},{20,3},{21,4},{22,5},{23,6},{24,7},{25,8},{26... | collective-permute-start | bytes 98312 | tf_op jit(solution)/shard_map/ppermute | solution.py:13
  13.3 1.9 collective-permute-start.1
  15.2 1.9 collective-permute-start.2
  17.1 6.6 %collective-permute-start.3 = (bf16[16,8,128]{2,1,0:T(8,128)(2,1)}, bf16[16,8,128]{2,1,0:T(8,128)(2,1)}, u32[]{:S(2)}, u32[]{:S(2)}) collective-permute-start(bf16[16,8,128]{2,1,0:T(8,128)(2,1)} %get-tuple-element.51), channel_id=1, source_target_pairs={{1,0},{2,1},{3,2},{4,3},{5,4},{6,5},{7,6},{8,7},{9,8},{10,9},{11,1... | collective-permute-start | bytes 98312 | tf_op jit(solution)/shard_map/ppermute | solution.py:13
  23.8 1.9 collective-permute-start.4
  28.7 7.6 %collective-permute-start.5 = (bf16[16,8,128]{2,1,0:T(8,128)(2,1)}, bf16[16,8,128]{2,1,0:T(8,128)(2,1)S(1)}, u32[]{:S(2)}, u32[]{:S(2)}) collective-permute-start(bf16[16,8,128]{2,1,0:T(8,128)(2,1)} %get-tuple-element.49), channel_id=1, source_target_pairs={{0,15},{1,16},{2,17},{3,18},{4,19},{5,20},{6,21},{7,22},{8,23},{9,... | collective-permute-start | bytes 98312 | tf_op jit(solution)/shard_map/ppermute | solution.py:13
  37.1 2.7 collective-permute-start.6
  40.7 1.9 collective-permute-start.7
  43.8 8.4 %collective-permute-done.7 = bf16[16,8,128]{2,1,0:T(8,128)(2,1)S(1)} collective-permute-done((bf16[16,8,128]{2,1,0:T(8,128)(2,1)}, bf16[16,8,128]{2,1,0:T(8,128)(2,1)S(1)}, u32[]{:S(2)}, u32[]{:S(2)}) %collective-permute-start.7) | collective-permute-done | bytes 32800 | tf_op jit(solution)/shard_map/ppermute | solution.py:13
  53.0 2.6 gather_fusion.1
  55.6 5.9 %convolution_bitcast_fusion.3 = f32[64,8,128]{2,1,0:T(8,128)S(1)} fusion(bf16[64,4,128,128]{3,2,1,0:T(8,128)(2,1)} %param.8, bf16[64,4,8,128]{3,2,1,0:T(8,128)(2,1)} %bitcast.295, pred[64,4]{1,0:T(8,128)(4,1)S(1)} %copy.36), kind=kOutput, calls=%fused_computation.20 | convolution fusion | flops 67371008 | bytes 9175296 | tf_op jit(solution)/shard_map/efij,efrj->eri/dot_general | solution.py:80
  66.1 1.9 collective-permute-start.8
  68.0 1.9 collective-permute-start.9
  69.9 3.2 collective-permute-start.10
  73.1 5.3 %collective-permute-start.11 = (bf16[16,8,128]{2,1,0:T(8,128)(2,1)S(1)}, bf16[16,8,128]{2,1,0:T(8,128)(2,1)S(1)}, u32[]{:S(2)}, u32[]{:S(2)}) collective-permute-start(bf16[16,8,128]{2,1,0:T(8,128)(2,1)S(1)} %get-tuple-element.43), channel_id=1, source_target_pairs={{1,0},{2,1},{3,2},{4,3},{5,4},{6,5},{7,6},{8,7},{9,8},{10,9},{11,1... | collective-permute-start | bytes 98312 | tf_op jit(solution)/shard_map/ppermute | solution.py:13
  78.5 1.9 collective-permute-start.12
  80.4 7.6 %collective-permute-start.13 = (bf16[16,8,128]{2,1,0:T(8,128)(2,1)S(1)}, bf16[16,8,128]{2,1,0:T(8,128)(2,1)S(1)}, u32[]{:S(2)}, u32[]{:S(2)}) collective-permute-start(bf16[16,8,128]{2,1,0:T(8,128)(2,1)S(1)} %get-tuple-element.41), channel_id=1, source_target_pairs={{0,15},{1,16},{2,17},{3,18},{4,19},{5,20},{6,21},{7,22},{8,23},{9,... | collective-permute-start | bytes 98312 | tf_op jit(solution)/shard_map/ppermute | solution.py:13
  88.0 2.7 collective-permute-start.14
  90.8 1.9 collective-permute-start.15
  94.5 7.8 %collective-permute-done.15 = bf16[16,8,128]{2,1,0:T(8,128)(2,1)S(1)} collective-permute-done((bf16[16,8,128]{2,1,0:T(8,128)(2,1)S(1)}, bf16[16,8,128]{2,1,0:T(8,128)(2,1)S(1)}, u32[]{:S(2)}, u32[]{:S(2)}) %collective-permute-start.15) | collective-permute-done | bytes 32800 | tf_op jit(solution)/shard_map/ppermute | solution.py:13
  103.1 2.6 gather_fusion.3
  105.7 5.9 %convolution_bitcast_fusion.2 = f32[64,8,128]{2,1,0:T(8,128)S(1)} fusion(bf16[64,4,128,128]{3,2,1,0:T(8,128)(2,1)} %param.8, bf16[64,4,8,128]{3,2,1,0:T(8,128)(2,1)} %bitcast.296, pred[64,4]{1,0:T(8,128)(4,1)S(1)} %copy.36), kind=kOutput, calls=%fused_computation.17 | convolution fusion | flops 67371008 | bytes 9175296 | tf_op jit(solution)/shard_map/efij,efrj->eri/dot_general | solution.py:80
  116.1 1.9 collective-permute-start.16
  120.6 3.0 collective-permute-start.18
  123.6 5.3 %collective-permute-start.19 = (bf16[16,8,128]{2,1,0:T(8,128)(2,1)S(1)}, bf16[16,8,128]{2,1,0:T(8,128)(2,1)S(1)}, u32[]{:S(2)}, u32[]{:S(2)}) collective-permute-start(bf16[16,8,128]{2,1,0:T(8,128)(2,1)S(1)} %get-tuple-element.35), channel_id=1, source_target_pairs={{1,0},{2,1},{3,2},{4,3},{5,4},{6,5},{7,6},{8,7},{9,8},{10,9},{11,1... | collective-permute-start | bytes 98312 | tf_op jit(solution)/shard_map/ppermute | solution.py:13
  128.9 1.9 collective-permute-start.20
  130.9 7.7 %collective-permute-start.21 = (bf16[16,8,128]{2,1,0:T(8,128)(2,1)S(1)}, bf16[16,8,128]{2,1,0:T(8,128)(2,1)S(1)}, u32[]{:S(2)}, u32[]{:S(2)}) collective-permute-start(bf16[16,8,128]{2,1,0:T(8,128)(2,1)S(1)} %get-tuple-element.33), channel_id=1, source_target_pairs={{0,15},{1,16},{2,17},{3,18},{4,19},{5,20},{6,21},{7,22},{8,23},{9,... | collective-permute-start | bytes 98312 | tf_op jit(solution)/shard_map/ppermute | solution.py:13
  138.7 2.7 collective-permute-start.22
  141.5 1.9 collective-permute-start.23
  145.1 7.9 %collective-permute-done.23 = bf16[16,8,128]{2,1,0:T(8,128)(2,1)S(1)} collective-permute-done((bf16[16,8,128]{2,1,0:T(8,128)(2,1)S(1)}, bf16[16,8,128]{2,1,0:T(8,128)(2,1)S(1)}, u32[]{:S(2)}, u32[]{:S(2)}) %collective-permute-start.23) | collective-permute-done | bytes 32800 | tf_op jit(solution)/shard_map/ppermute | solution.py:13
  153.8 2.6 gather_fusion.5
  156.4 5.9 %convolution_bitcast_fusion.1 = f32[64,8,128]{2,1,0:T(8,128)S(1)} fusion(bf16[64,4,128,128]{3,2,1,0:T(8,128)(2,1)} %param.8, bf16[64,4,8,128]{3,2,1,0:T(8,128)(2,1)} %bitcast.297, pred[64,4]{1,0:T(8,128)(4,1)S(1)} %copy.36), kind=kOutput, calls=%fused_computation.14 | convolution fusion | flops 67371008 | bytes 9175296 | tf_op jit(solution)/shard_map/efij,efrj->eri/dot_general | solution.py:80
  166.8 1.9 collective-permute-start.24
  171.2 2.7 collective-permute-start.26
  173.9 5.3 %collective-permute-start.27 = (bf16[16,8,128]{2,1,0:T(8,128)(2,1)S(1)}, bf16[16,8,128]{2,1,0:T(8,128)(2,1)S(1)}, u32[]{:S(2)}, u32[]{:S(2)}) collective-permute-start(bf16[16,8,128]{2,1,0:T(8,128)(2,1)S(1)} %get-tuple-element.27), channel_id=1, source_target_pairs={{1,0},{2,1},{3,2},{4,3},{5,4},{6,5},{7,6},{8,7},{9,8},{10,9},{11,1... | collective-permute-start | bytes 98312 | tf_op jit(solution)/shard_map/ppermute | solution.py:13
  179.3 1.9 collective-permute-start.28
  181.2 8.1 %collective-permute-start.29 = (bf16[16,8,128]{2,1,0:T(8,128)(2,1)S(1)}, bf16[16,8,128]{2,1,0:T(8,128)(2,1)S(1)}, u32[]{:S(2)}, u32[]{:S(2)}) collective-permute-start(bf16[16,8,128]{2,1,0:T(8,128)(2,1)S(1)} %get-tuple-element.25), channel_id=1, source_target_pairs={{0,15},{1,16},{2,17},{3,18},{4,19},{5,20},{6,21},{7,22},{8,23},{9,... | collective-permute-start | bytes 98312 | tf_op jit(solution)/shard_map/ppermute | solution.py:13
  189.3 2.7 collective-permute-start.30
  192.1 2.1 collective-permute-start.31
  195.8 7.9 %collective-permute-done.31 = bf16[16,8,128]{2,1,0:T(8,128)(2,1)S(1)} collective-permute-done((bf16[16,8,128]{2,1,0:T(8,128)(2,1)S(1)}, bf16[16,8,128]{2,1,0:T(8,128)(2,1)S(1)}, u32[]{:S(2)}, u32[]{:S(2)}) %collective-permute-start.31) | collective-permute-done | bytes 32800 | tf_op jit(solution)/shard_map/ppermute | solution.py:13
  204.4 2.6 gather_fusion.7
  207.0 5.9 %convolution_bitcast_fusion = f32[64,8,128]{2,1,0:T(8,128)S(1)} fusion(bf16[64,4,128,128]{3,2,1,0:T(8,128)(2,1)} %param.8, bf16[64,4,8,128]{3,2,1,0:T(8,128)(2,1)} %bitcast.294, pred[64,4]{1,0:T(8,128)(4,1)S(1)} %copy.36), kind=kOutput, calls=%fused_computation.10 | convolution fusion | flops 67371008 | bytes 9175296 | tf_op jit(solution)/shard_map/efij,efrj->eri/dot_general | solution.py:80
  214.8 4.9 %fusion.7 = f32[8,5,5]{1,2,0:T(8,128)S(1)} fusion(f32[5,64,8,128]{3,2,1,0:T(8,128)S(1)} %get-tuple-element.61), kind=kOutput, calls=%fused_computation.23 | convolution fusion | flops 19660800 | bytes 1311520 | tf_op jit(solution)/shard_map/icrn,jcrn->rij/dot_general | solution.py:85
  219.8 45.8 %psum.14 = f32[8,5,5]{1,2,0:T(8,128)S(1)} all-reduce(f32[8,5,5]{1,2,0:T(8,128)S(1)} %fusion.7), channel_id=1, replica_groups=mesh['gx'=16,'gy'=16] {'gx'}, use_global_device_ids=true, to_apply=%region_0.1 | all-reduce | flops 200 | bytes 1600 | tf_op jit(solution)/shard_map/psum | solution.py:86
  265.5 69.8 %psum.15 = f32[8,5,5]{1,2,0:T(8,128)S(1)} all-reduce(f32[8,5,5]{1,2,0:T(8,128)S(1)} %psum.14), channel_id=1, replica_groups=mesh['gx'=16,'gy'=16] {'gy'}, use_global_device_ids=true, to_apply=%region_1.2 | all-reduce | flops 200 | bytes 1600 | tf_op jit(solution)/shard_map/psum | solution.py:86
  335.6 3.0 custom-call.4
  341.1 2.5 fusion.12
  344.5 2.5 fusion.10
  (149 shorter events, 44.2 us)
Async XLA Ops:
  0.6 60.9 %copy-start = (bf16[64,128,128]{2,1,0:T(8,128)(2,1)S(1)}, bf16[64,128,128]{2,1,0:T(8,128)(2,1)}, u32[]{:S(2)}) copy-start(bf16[64,128,128]{2,1,0:T(8,128)(2,1)} %param.7) | copy-start | bytes 6291460
  0.6 26.8 %copy-start.11 = (s32[64,4]{0,1:T(4,128)S(1)}, s32[64,4]{0,1:T(4,128)}, u32[]{:S(2)}) copy-start(s32[64,4]{0,1:T(4,128)} %param.9) | copy-start | bytes 3076
  2.9 25.1 %copy-start.6 = (f32[64]{0:T(128)}, f32[64]{0:T(128)S(1)}, u32[]{:S(2)}) copy-start(f32[64]{0:T(128)S(1)} %compare_convert_fusion) | copy-start | bytes 772
  3.9 19.9 %copy-start.5 = (pred[1,9,16]{2,1,0:T(8,128)(4,1)}, pred[1,9,16]{2,1,0:T(8,128)(4,1)S(1)}, u32[]{:S(2)}) copy-start(pred[1,9,16]{2,1,0:T(8,128)(4,1)S(1)} %copy.69) | copy-start | bytes 436
  6.6 22.1 %collective-permute-start = (bf16[16,8,128]{2,1,0:T(8,128)(2,1)}, bf16[16,8,128]{2,1,0:T(8,128)(2,1)}, u32[]{:S(2)}, u32[]{:S(2)}) collective-permute-start(bf16[16,8,128]{2,1,0:T(8,128)(2,1)} %get-tuple-element.54), channel_id=1, source_target_pairs={{17,0},{18,1},{19,2},{20,3},{21,4},{22,5},{23,6},{24,7},{25,8},{26... | collective-permute-start | bytes 98312 | tf_op jit(solution)/shard_map/ppermute | solution.py:13
  13.3 23.9 %collective-permute-start.1 = (bf16[16,8,128]{2,1,0:T(8,128)(2,1)}, bf16[16,8,128]{2,1,0:T(8,128)(2,1)}, u32[]{:S(2)}, u32[]{:S(2)}) collective-permute-start(bf16[16,8,128]{2,1,0:T(8,128)(2,1)} %get-tuple-element.53), channel_id=1, source_target_pairs={{16,0},{17,1},{18,2},{19,3},{20,4},{21,5},{22,6},{23,7},{24,8},{25... | collective-permute-start | bytes 98312 | tf_op jit(solution)/shard_map/ppermute | solution.py:13
  15.2 25.5 %collective-permute-start.2 = (bf16[16,8,128]{2,1,0:T(8,128)(2,1)}, bf16[16,8,128]{2,1,0:T(8,128)(2,1)}, u32[]{:S(2)}, u32[]{:S(2)}) collective-permute-start(bf16[16,8,128]{2,1,0:T(8,128)(2,1)} %get-tuple-element.52), channel_id=1, source_target_pairs={{15,0},{16,1},{17,2},{18,3},{19,4},{20,5},{21,6},{22,7},{23,8},{24... | collective-permute-start | bytes 98312 | tf_op jit(solution)/shard_map/ppermute | solution.py:13
  17.1 25.5 %collective-permute-start.3 = (bf16[16,8,128]{2,1,0:T(8,128)(2,1)}, bf16[16,8,128]{2,1,0:T(8,128)(2,1)}, u32[]{:S(2)}, u32[]{:S(2)}) collective-permute-start(bf16[16,8,128]{2,1,0:T(8,128)(2,1)} %get-tuple-element.51), channel_id=1, source_target_pairs={{1,0},{2,1},{3,2},{4,3},{5,4},{6,5},{7,6},{8,7},{9,8},{10,9},{11,1... | collective-permute-start | bytes 98312 | tf_op jit(solution)/shard_map/ppermute | solution.py:13
  23.8 19.7 %collective-permute-start.4 = (bf16[16,8,128]{2,1,0:T(8,128)(2,1)}, bf16[16,8,128]{2,1,0:T(8,128)(2,1)}, u32[]{:S(2)}, u32[]{:S(2)}) collective-permute-start(bf16[16,8,128]{2,1,0:T(8,128)(2,1)} %get-tuple-element.50), channel_id=1, source_target_pairs={{0,1},{1,2},{2,3},{3,4},{4,5},{5,6},{6,7},{7,8},{8,9},{9,10},{10,1... | collective-permute-start | bytes 98312 | tf_op jit(solution)/shard_map/ppermute | solution.py:13
  28.7 14.7 %collective-permute-start.5 = (bf16[16,8,128]{2,1,0:T(8,128)(2,1)}, bf16[16,8,128]{2,1,0:T(8,128)(2,1)S(1)}, u32[]{:S(2)}, u32[]{:S(2)}) collective-permute-start(bf16[16,8,128]{2,1,0:T(8,128)(2,1)} %get-tuple-element.49), channel_id=1, source_target_pairs={{0,15},{1,16},{2,17},{3,18},{4,19},{5,20},{6,21},{7,22},{8,23},{9,... | collective-permute-start | bytes 98312 | tf_op jit(solution)/shard_map/ppermute | solution.py:13
  37.1 6.7 %collective-permute-start.6 = (bf16[16,8,128]{2,1,0:T(8,128)(2,1)}, bf16[16,8,128]{2,1,0:T(8,128)(2,1)S(1)}, u32[]{:S(2)}, u32[]{:S(2)}) collective-permute-start(bf16[16,8,128]{2,1,0:T(8,128)(2,1)} %get-tuple-element.48), channel_id=1, source_target_pairs={{0,16},{1,17},{2,18},{3,19},{4,20},{5,21},{6,22},{7,23},{8,24},{9,... | collective-permute-start | bytes 98312 | tf_op jit(solution)/shard_map/ppermute | solution.py:13
  40.7 11.6 %collective-permute-start.7 = (bf16[16,8,128]{2,1,0:T(8,128)(2,1)}, bf16[16,8,128]{2,1,0:T(8,128)(2,1)S(1)}, u32[]{:S(2)}, u32[]{:S(2)}) collective-permute-start(bf16[16,8,128]{2,1,0:T(8,128)(2,1)} %get-tuple-element.47), channel_id=1, source_target_pairs={{0,17},{1,18},{2,19},{3,20},{4,21},{5,22},{6,23},{7,24},{8,25},{9,... | collective-permute-start | bytes 98312 | tf_op jit(solution)/shard_map/ppermute | solution.py:13
  55.6 5.9 %copy-start.7 = (f32[64]{0:T(128)S(1)}, f32[64]{0:T(128)}, u32[]{:S(2)}) copy-start(f32[64]{0:T(128)} %copy-done.6) | copy-start | bytes 772
  62.7 0.7 copy-start.2
  66.1 14.3 %collective-permute-start.8 = (bf16[16,8,128]{2,1,0:T(8,128)(2,1)S(1)}, bf16[16,8,128]{2,1,0:T(8,128)(2,1)S(1)}, u32[]{:S(2)}, u32[]{:S(2)}) collective-permute-start(bf16[16,8,128]{2,1,0:T(8,128)(2,1)S(1)} %get-tuple-element.46), channel_id=1, source_target_pairs={{17,0},{18,1},{19,2},{20,3},{21,4},{22,5},{23,6},{24,7},{25,8},{26... | collective-permute-start | bytes 98312 | tf_op jit(solution)/shard_map/ppermute | solution.py:13
  68.0 20.0 %collective-permute-start.9 = (bf16[16,8,128]{2,1,0:T(8,128)(2,1)S(1)}, bf16[16,8,128]{2,1,0:T(8,128)(2,1)S(1)}, u32[]{:S(2)}, u32[]{:S(2)}) collective-permute-start(bf16[16,8,128]{2,1,0:T(8,128)(2,1)S(1)} %get-tuple-element.45), channel_id=1, source_target_pairs={{16,0},{17,1},{18,2},{19,3},{20,4},{21,5},{22,6},{23,7},{24,8},{25... | collective-permute-start | bytes 98312 | tf_op jit(solution)/shard_map/ppermute | solution.py:13
  69.9 20.9 %collective-permute-start.10 = (bf16[16,8,128]{2,1,0:T(8,128)(2,1)S(1)}, bf16[16,8,128]{2,1,0:T(8,128)(2,1)S(1)}, u32[]{:S(2)}, u32[]{:S(2)}) collective-permute-start(bf16[16,8,128]{2,1,0:T(8,128)(2,1)S(1)} %get-tuple-element.44), channel_id=1, source_target_pairs={{15,0},{16,1},{17,2},{18,3},{19,4},{20,5},{21,6},{22,7},{23,8},{24... | collective-permute-start | bytes 98312 | tf_op jit(solution)/shard_map/ppermute | solution.py:13
  73.1 19.7 %collective-permute-start.11 = (bf16[16,8,128]{2,1,0:T(8,128)(2,1)S(1)}, bf16[16,8,128]{2,1,0:T(8,128)(2,1)S(1)}, u32[]{:S(2)}, u32[]{:S(2)}) collective-permute-start(bf16[16,8,128]{2,1,0:T(8,128)(2,1)S(1)} %get-tuple-element.43), channel_id=1, source_target_pairs={{1,0},{2,1},{3,2},{4,3},{5,4},{6,5},{7,6},{8,7},{9,8},{10,9},{11,1... | collective-permute-start | bytes 98312 | tf_op jit(solution)/shard_map/ppermute | solution.py:13
  78.5 14.4 %collective-permute-start.12 = (bf16[16,8,128]{2,1,0:T(8,128)(2,1)S(1)}, bf16[16,8,128]{2,1,0:T(8,128)(2,1)S(1)}, u32[]{:S(2)}, u32[]{:S(2)}) collective-permute-start(bf16[16,8,128]{2,1,0:T(8,128)(2,1)S(1)} %get-tuple-element.42), channel_id=1, source_target_pairs={{0,1},{1,2},{2,3},{3,4},{4,5},{5,6},{6,7},{7,8},{8,9},{9,10},{10,1... | collective-permute-start | bytes 98312 | tf_op jit(solution)/shard_map/ppermute | solution.py:13
  80.4 12.5 %collective-permute-start.13 = (bf16[16,8,128]{2,1,0:T(8,128)(2,1)S(1)}, bf16[16,8,128]{2,1,0:T(8,128)(2,1)S(1)}, u32[]{:S(2)}, u32[]{:S(2)}) collective-permute-start(bf16[16,8,128]{2,1,0:T(8,128)(2,1)S(1)} %get-tuple-element.41), channel_id=1, source_target_pairs={{0,15},{1,16},{2,17},{3,18},{4,19},{5,20},{6,21},{7,22},{8,23},{9,... | collective-permute-start | bytes 98312 | tf_op jit(solution)/shard_map/ppermute | solution.py:13
  88.0 6.4 %collective-permute-start.14 = (bf16[16,8,128]{2,1,0:T(8,128)(2,1)S(1)}, bf16[16,8,128]{2,1,0:T(8,128)(2,1)S(1)}, u32[]{:S(2)}, u32[]{:S(2)}) collective-permute-start(bf16[16,8,128]{2,1,0:T(8,128)(2,1)S(1)} %get-tuple-element.40), channel_id=1, source_target_pairs={{0,16},{1,17},{2,18},{3,19},{4,20},{5,21},{6,22},{7,23},{8,24},{9,... | collective-permute-start | bytes 98312 | tf_op jit(solution)/shard_map/ppermute | solution.py:13
  90.8 11.5 %collective-permute-start.15 = (bf16[16,8,128]{2,1,0:T(8,128)(2,1)S(1)}, bf16[16,8,128]{2,1,0:T(8,128)(2,1)S(1)}, u32[]{:S(2)}, u32[]{:S(2)}) collective-permute-start(bf16[16,8,128]{2,1,0:T(8,128)(2,1)S(1)} %get-tuple-element.39), channel_id=1, source_target_pairs={{0,17},{1,18},{2,19},{3,20},{4,21},{5,22},{6,23},{7,24},{8,25},{9,... | collective-permute-start | bytes 98312 | tf_op jit(solution)/shard_map/ppermute | solution.py:13
  105.7 5.9 %copy-start.8 = (f32[64]{0:T(128)S(1)}, f32[64]{0:T(128)}, u32[]{:S(2)}) copy-start(f32[64]{0:T(128)} %copy-done.6) | copy-start | bytes 772
  112.8 0.7 copy-start.3
  116.1 14.7 %collective-permute-start.16 = (bf16[16,8,128]{2,1,0:T(8,128)(2,1)S(1)}, bf16[16,8,128]{2,1,0:T(8,128)(2,1)S(1)}, u32[]{:S(2)}, u32[]{:S(2)}) collective-permute-start(bf16[16,8,128]{2,1,0:T(8,128)(2,1)S(1)} %get-tuple-element.38), channel_id=1, source_target_pairs={{17,0},{18,1},{19,2},{20,3},{21,4},{22,5},{23,6},{24,7},{25,8},{26... | collective-permute-start | bytes 98312 | tf_op jit(solution)/shard_map/ppermute | solution.py:13
  118.6 20.0 %collective-permute-start.17 = (bf16[16,8,128]{2,1,0:T(8,128)(2,1)S(1)}, bf16[16,8,128]{2,1,0:T(8,128)(2,1)S(1)}, u32[]{:S(2)}, u32[]{:S(2)}) collective-permute-start(bf16[16,8,128]{2,1,0:T(8,128)(2,1)S(1)} %get-tuple-element.37), channel_id=1, source_target_pairs={{16,0},{17,1},{18,2},{19,3},{20,4},{21,5},{22,6},{23,7},{24,8},{25... | collective-permute-start | bytes 98312 | tf_op jit(solution)/shard_map/ppermute | solution.py:13
  120.6 20.9 %collective-permute-start.18 = (bf16[16,8,128]{2,1,0:T(8,128)(2,1)S(1)}, bf16[16,8,128]{2,1,0:T(8,128)(2,1)S(1)}, u32[]{:S(2)}, u32[]{:S(2)}) collective-permute-start(bf16[16,8,128]{2,1,0:T(8,128)(2,1)S(1)} %get-tuple-element.36), channel_id=1, source_target_pairs={{15,0},{16,1},{17,2},{18,3},{19,4},{20,5},{21,6},{22,7},{23,8},{24... | collective-permute-start | bytes 98312 | tf_op jit(solution)/shard_map/ppermute | solution.py:13
  123.6 19.8 %collective-permute-start.19 = (bf16[16,8,128]{2,1,0:T(8,128)(2,1)S(1)}, bf16[16,8,128]{2,1,0:T(8,128)(2,1)S(1)}, u32[]{:S(2)}, u32[]{:S(2)}) collective-permute-start(bf16[16,8,128]{2,1,0:T(8,128)(2,1)S(1)} %get-tuple-element.35), channel_id=1, source_target_pairs={{1,0},{2,1},{3,2},{4,3},{5,4},{6,5},{7,6},{8,7},{9,8},{10,9},{11,1... | collective-permute-start | bytes 98312 | tf_op jit(solution)/shard_map/ppermute | solution.py:13
  128.9 14.5 %collective-permute-start.20 = (bf16[16,8,128]{2,1,0:T(8,128)(2,1)S(1)}, bf16[16,8,128]{2,1,0:T(8,128)(2,1)S(1)}, u32[]{:S(2)}, u32[]{:S(2)}) collective-permute-start(bf16[16,8,128]{2,1,0:T(8,128)(2,1)S(1)} %get-tuple-element.34), channel_id=1, source_target_pairs={{0,1},{1,2},{2,3},{3,4},{4,5},{5,6},{6,7},{7,8},{8,9},{9,10},{10,1... | collective-permute-start | bytes 98312 | tf_op jit(solution)/shard_map/ppermute | solution.py:13
  130.9 12.6 %collective-permute-start.21 = (bf16[16,8,128]{2,1,0:T(8,128)(2,1)S(1)}, bf16[16,8,128]{2,1,0:T(8,128)(2,1)S(1)}, u32[]{:S(2)}, u32[]{:S(2)}) collective-permute-start(bf16[16,8,128]{2,1,0:T(8,128)(2,1)S(1)} %get-tuple-element.33), channel_id=1, source_target_pairs={{0,15},{1,16},{2,17},{3,18},{4,19},{5,20},{6,21},{7,22},{8,23},{9,... | collective-permute-start | bytes 98312 | tf_op jit(solution)/shard_map/ppermute | solution.py:13
  138.7 6.4 %collective-permute-start.22 = (bf16[16,8,128]{2,1,0:T(8,128)(2,1)S(1)}, bf16[16,8,128]{2,1,0:T(8,128)(2,1)S(1)}, u32[]{:S(2)}, u32[]{:S(2)}) collective-permute-start(bf16[16,8,128]{2,1,0:T(8,128)(2,1)S(1)} %get-tuple-element.32), channel_id=1, source_target_pairs={{0,16},{1,17},{2,18},{3,19},{4,20},{5,21},{6,22},{7,23},{8,24},{9,... | collective-permute-start | bytes 98312 | tf_op jit(solution)/shard_map/ppermute | solution.py:13
  141.5 11.5 %collective-permute-start.23 = (bf16[16,8,128]{2,1,0:T(8,128)(2,1)S(1)}, bf16[16,8,128]{2,1,0:T(8,128)(2,1)S(1)}, u32[]{:S(2)}, u32[]{:S(2)}) collective-permute-start(bf16[16,8,128]{2,1,0:T(8,128)(2,1)S(1)} %get-tuple-element.31), channel_id=1, source_target_pairs={{0,17},{1,18},{2,19},{3,20},{4,21},{5,22},{6,23},{7,24},{8,25},{9,... | collective-permute-start | bytes 98312 | tf_op jit(solution)/shard_map/ppermute | solution.py:13
  156.4 5.9 %copy-start.9 = (f32[64]{0:T(128)S(1)}, f32[64]{0:T(128)}, u32[]{:S(2)}) copy-start(f32[64]{0:T(128)} %copy-done.6) | copy-start | bytes 772
  163.5 0.7 copy-start.4
  166.8 14.4 %collective-permute-start.24 = (bf16[16,8,128]{2,1,0:T(8,128)(2,1)S(1)}, bf16[16,8,128]{2,1,0:T(8,128)(2,1)S(1)}, u32[]{:S(2)}, u32[]{:S(2)}) collective-permute-start(bf16[16,8,128]{2,1,0:T(8,128)(2,1)S(1)} %get-tuple-element.30), channel_id=1, source_target_pairs={{17,0},{18,1},{19,2},{20,3},{21,4},{22,5},{23,6},{24,7},{25,8},{26... | collective-permute-start | bytes 98312 | tf_op jit(solution)/shard_map/ppermute | solution.py:13
  169.3 20.0 %collective-permute-start.25 = (bf16[16,8,128]{2,1,0:T(8,128)(2,1)S(1)}, bf16[16,8,128]{2,1,0:T(8,128)(2,1)S(1)}, u32[]{:S(2)}, u32[]{:S(2)}) collective-permute-start(bf16[16,8,128]{2,1,0:T(8,128)(2,1)S(1)} %get-tuple-element.29), channel_id=1, source_target_pairs={{16,0},{17,1},{18,2},{19,3},{20,4},{21,5},{22,6},{23,7},{24,8},{25... | collective-permute-start | bytes 98312 | tf_op jit(solution)/shard_map/ppermute | solution.py:13
  171.2 20.9 %collective-permute-start.26 = (bf16[16,8,128]{2,1,0:T(8,128)(2,1)S(1)}, bf16[16,8,128]{2,1,0:T(8,128)(2,1)S(1)}, u32[]{:S(2)}, u32[]{:S(2)}) collective-permute-start(bf16[16,8,128]{2,1,0:T(8,128)(2,1)S(1)} %get-tuple-element.28), channel_id=1, source_target_pairs={{15,0},{16,1},{17,2},{18,3},{19,4},{20,5},{21,6},{22,7},{23,8},{24... | collective-permute-start | bytes 98312 | tf_op jit(solution)/shard_map/ppermute | solution.py:13
  173.9 20.3 %collective-permute-start.27 = (bf16[16,8,128]{2,1,0:T(8,128)(2,1)S(1)}, bf16[16,8,128]{2,1,0:T(8,128)(2,1)S(1)}, u32[]{:S(2)}, u32[]{:S(2)}) collective-permute-start(bf16[16,8,128]{2,1,0:T(8,128)(2,1)S(1)} %get-tuple-element.27), channel_id=1, source_target_pairs={{1,0},{2,1},{3,2},{4,3},{5,4},{6,5},{7,6},{8,7},{9,8},{10,9},{11,1... | collective-permute-start | bytes 98312 | tf_op jit(solution)/shard_map/ppermute | solution.py:13
  179.3 15.0 %collective-permute-start.28 = (bf16[16,8,128]{2,1,0:T(8,128)(2,1)S(1)}, bf16[16,8,128]{2,1,0:T(8,128)(2,1)S(1)}, u32[]{:S(2)}, u32[]{:S(2)}) collective-permute-start(bf16[16,8,128]{2,1,0:T(8,128)(2,1)S(1)} %get-tuple-element.26), channel_id=1, source_target_pairs={{0,1},{1,2},{2,3},{3,4},{4,5},{5,6},{6,7},{7,8},{8,9},{9,10},{10,1... | collective-permute-start | bytes 98312 | tf_op jit(solution)/shard_map/ppermute | solution.py:13
  181.2 13.1 %collective-permute-start.29 = (bf16[16,8,128]{2,1,0:T(8,128)(2,1)S(1)}, bf16[16,8,128]{2,1,0:T(8,128)(2,1)S(1)}, u32[]{:S(2)}, u32[]{:S(2)}) collective-permute-start(bf16[16,8,128]{2,1,0:T(8,128)(2,1)S(1)} %get-tuple-element.25), channel_id=1, source_target_pairs={{0,15},{1,16},{2,17},{3,18},{4,19},{5,20},{6,21},{7,22},{8,23},{9,... | collective-permute-start | bytes 98312 | tf_op jit(solution)/shard_map/ppermute | solution.py:13
  189.3 6.4 %collective-permute-start.30 = (bf16[16,8,128]{2,1,0:T(8,128)(2,1)S(1)}, bf16[16,8,128]{2,1,0:T(8,128)(2,1)S(1)}, u32[]{:S(2)}, u32[]{:S(2)}) collective-permute-start(bf16[16,8,128]{2,1,0:T(8,128)(2,1)S(1)} %get-tuple-element.24), channel_id=1, source_target_pairs={{0,16},{1,17},{2,18},{3,19},{4,20},{5,21},{6,22},{7,23},{8,24},{9,... | collective-permute-start | bytes 98312 | tf_op jit(solution)/shard_map/ppermute | solution.py:13
  192.1 11.5 %collective-permute-start.31 = (bf16[16,8,128]{2,1,0:T(8,128)(2,1)S(1)}, bf16[16,8,128]{2,1,0:T(8,128)(2,1)S(1)}, u32[]{:S(2)}, u32[]{:S(2)}) collective-permute-start(bf16[16,8,128]{2,1,0:T(8,128)(2,1)S(1)} %get-tuple-element.23), channel_id=1, source_target_pairs={{0,17},{1,18},{2,19},{3,20},{4,21},{5,22},{6,23},{7,24},{8,25},{9,... | collective-permute-start | bytes 98312 | tf_op jit(solution)/shard_map/ppermute | solution.py:13
  207.0 5.9 %copy-start.10 = (f32[64]{0:T(128)S(1)}, f32[64]{0:T(128)}, u32[]{:S(2)}) copy-start(f32[64]{0:T(128)} %copy-done.6) | copy-start | bytes 772
  214.8 123.8 %copy-start.13 = (pred[4,4]{1,0:T(4,128)(4,1)S(1)}, pred[4,4]{1,0:T(4,128)(4,1)}, u32[]{:S(2)}) copy-start(pred[4,4]{1,0:T(4,128)(4,1)} %iota_compare_fusion) | copy-start | bytes 52
  214.8 124.0 %copy-start.12 = (pred[4,4]{1,0:T(4,128)(4,1)S(1)}, pred[4,4]{1,0:T(4,128)(4,1)}, u32[]{:S(2)}) copy-start(pred[4,4]{1,0:T(4,128)(4,1)} %iota_compare_fusion.1) | copy-start | bytes 52
  341.1 5.9 %copy-start.1 = (f32[64,8,128]{2,1,0:T(8,128)S(1)}, f32[64,8,128]{2,1,0:T(8,128)}, u32[]{:S(2)}) copy-start(f32[64,8,128]{2,1,0:T(8,128)} %param.6) | copy-start | bytes 786436
